TPU v7x, 32 devices: a whole 2x2x4 slice. The times are simulated.
32 devices in a mesh: rows: 4 (over y, x), cols: 8 (over z, core).
Axes of the slice: x: 2, y: 2, z: 4, core: 2. Of those that a mesh axis runs over, the one named last changes fastest.
Arguments:
- embeddings: bfloat16 [4096, 768], P(('rows', 'cols')), may hold values from -6 to 6
- document_cluster_index: int32 [4096], P(('rows', 'cols')), may hold values from 0 to 63, as said below
Outputs:
- max_similarity: float32 [4096], P(('rows', 'cols'))
- histogram: float32 [128], replicated
Inputs may be any that keep to these rules, and one draw needn't show every extreme that they name: `document_cluster_index`: cluster r * 16 to (r + 1) * 16 - 1 form row group r. Each device's block of 128 documents names at most 64 documents of any one row group, and exactly 64 of one. The documents that the devices with one index along cols name for one row group hold at most 32 documents of any one cluster, and in every draw some such set holds exactly 32 of one cluster.
All inputs are finite; a program needn't handle non-finite values.
Results may differ from a plain program's by a relative error of at most 0.0014.
Values may be sent and summed in bfloat16 or wider, within the bound.
A program may use at most 64 MiB of HBM per device.

v0:
```python
import jax
import jax.numpy as jnp
from jax import lax
from jax.sharding import PartitionSpec as P

CAP = 64
GROUP_CLUSTERS = 16
BINS = 128


def from_partner(value, axis, bit):
    mask = 2**bit
    pairs = [(source, source ^ mask) for source in range(lax.axis_size(axis))]
    return lax.ppermute(value, axis, pairs)


def shards(embeddings, document_cluster_index):
    row_count = lax.axis_size("rows")
    col_count = lax.axis_size("cols")
    doc_count = embeddings.shape[0]
    width = embeddings.shape[1]
    slot_count = CAP * row_count
    values = embeddings.astype(jnp.float32)
    normed = (values * lax.rsqrt(jnp.sum(values * values, axis=1, keepdims=True) + 1e-06)).astype(
        jnp.bfloat16
    )
    owner_devices = document_cluster_index // GROUP_CLUSTERS
    within_cluster = (document_cluster_index % GROUP_CLUSTERS).astype(jnp.float32)
    onehot_rows = (
        owner_devices[:, None] == jnp.arange(row_count, dtype=jnp.int32)[None, :]
    ).astype(jnp.int32)
    slot_ranks = jnp.sum((jnp.cumsum(onehot_rows, axis=0) - 1) * onehot_rows, axis=1)
    places = owner_devices * CAP + slot_ranks
    outgoing = jnp.zeros((slot_count, width), jnp.bfloat16).at[places].set(normed)
    out_labels = (
        jnp.full((slot_count,), -1.0, jnp.float32)
        .at[places]
        .set(within_cluster)
        .astype(jnp.bfloat16)
    )
    resident, res_labels = (
        lax.all_to_all(outgoing, "rows", split_axis=0, concat_axis=0, tiled=True),
        lax.all_to_all(out_labels, "rows", split_axis=0, concat_axis=0, tiled=True),
    )
    home_labels = res_labels.astype(jnp.float32)
    partner_count = max(1, col_count // GROUP_CLUSTERS)
    owned_count = max(1, GROUP_CLUSTERS // col_count)
    slot_quota = 2 * slot_count // GROUP_CLUSTERS // partner_count
    send_total = col_count * owned_count * slot_quota
    local_cluster = res_labels.astype(jnp.int32)
    occupied = local_cluster >= 0
    onehot_clusters = (
        local_cluster[:, None] == jnp.arange(GROUP_CLUSTERS, dtype=jnp.int32)[None, :]
    ).astype(jnp.int32)
    cluster_rank = jnp.sum((jnp.cumsum(onehot_clusters, axis=0) - 1) * onehot_clusters, axis=1)
    member_slot = cluster_rank % partner_count
    cluster_depth = cluster_rank // partner_count
    destination = local_cluster // owned_count * partner_count + member_slot
    send_place = (
        destination * (owned_count * slot_quota)
        + local_cluster % owned_count * slot_quota
        + cluster_depth
    )
    send_place = jnp.where(occupied, send_place, send_total)
    send_rows = (
        jnp.zeros((send_total, width), jnp.bfloat16).at[send_place].set(resident, mode="drop")
    )
    send_labels = (
        jnp.full((send_total,), -1.0, jnp.float32)
        .at[send_place]
        .set(home_labels, mode="drop")
        .astype(jnp.bfloat16)
    )
    got_rows, got_labels = (
        lax.all_to_all(send_rows, "cols", split_axis=0, concat_axis=0, tiled=True),
        lax.all_to_all(send_labels, "cols", split_axis=0, concat_axis=0, tiled=True),
    )
    member_index = lax.axis_index("cols") % partner_count
    gathered_rows, gathered_labels = (got_rows, got_labels)
    for bit in range(partner_count.bit_length() - 1):
        other_rows, other_labels = from_partner((gathered_rows, gathered_labels), "cols", bit)
        upper = member_index // 2**bit % 2 == 1
        gathered_rows = jnp.where(
            upper,
            jnp.concatenate([other_rows, gathered_rows], axis=0),
            jnp.concatenate([gathered_rows, other_rows], axis=0),
        )
        gathered_labels = jnp.where(
            upper,
            jnp.concatenate([other_labels, gathered_labels], axis=0),
            jnp.concatenate([gathered_labels, other_labels], axis=0),
        )
    similarity_scores = lax.dot_general(
        got_rows, gathered_rows, (((1,), (1,)), ((), ())), preferred_element_type=jnp.float32
    )
    own_labels = got_labels.astype(jnp.float32)
    all_labels = gathered_labels.astype(jnp.float32)
    column_index = jnp.arange(gathered_rows.shape[0], dtype=jnp.int32)
    own_index = member_index * send_total + jnp.arange(send_total, dtype=jnp.int32)
    same_cluster = (own_labels[:, None] == all_labels[None, :]) & (own_labels[:, None] >= 0.0)
    same_cluster = same_cluster & (own_index[:, None] != column_index[None, :])
    best_owned = jnp.max(jnp.where(same_cluster, similarity_scores, -1.0), axis=1)
    came_back = lax.all_to_all(best_owned, "cols", split_axis=0, concat_axis=0, tiled=True)
    row_best = jnp.where(occupied, came_back[jnp.minimum(send_place, send_total - 1)], -1.0)
    answers = lax.all_to_all(row_best, "rows", split_axis=0, concat_axis=0, tiled=True)
    max_similarity = answers[places]
    bin_width = 2.0 / (BINS - 1)
    centers = -1.0 + jnp.arange(BINS, dtype=jnp.float32) * bin_width
    bin_weights = jax.nn.relu(1.0 - jnp.abs(max_similarity[:, None] - centers[None, :]) / bin_width)
    bin_totals = lax.psum(jnp.sum(bin_weights, axis=0), ("rows", "cols"))
    return (max_similarity, bin_totals / (doc_count * row_count * col_count))


def solution(mesh):
    placed = (P(("rows", "cols"), None), P(("rows", "cols")))
    return jax.shard_map(
        shards, mesh=mesh, in_specs=placed, out_specs=(P(("rows", "cols")), P()), check_vma=False
    )
```

profile of v0, /device:TPU:0, one launch (start us, length us, event | category | flops | bytes accessed | tf_op | source)
XLA Modules:
  0.0 120.5 jit_solution(5320224479067145139)
XLA Ops:
  0.6 0.7 fusion.19
  1.8 1.0 scatter_custom_fusion
  2.8 0.7 all_to_all.57
  3.5 5.2 %all-to-all-start = ((bf16[4,64,1]{1,2,0:T(2,128)(2,1)}), bf16[4,64,1]{1,2,0:T(2,128)(2,1)S(1)}, u32[]{:S(2)}, u32[]{:S(2)}) async-start(bf16[4,64,1]{1,2,0:T(2,128)(2,1)} %all_to_all.57), calls=%async_computation | async-start | bytes 4096 | tf_op jit(solution)/shard_map/all_to_all | solution.py:43
  8.8 1.9 %scatter_custom_fusion.2 = bf16[256,768]{1,0:T(8,128)(2,1)} fusion(s32[128]{0:T(128)S(1)} %compare_select_fusion.4, bf16[128,768]{1,0:T(8,128)(2,1)S(1)} %copy-done, f32[128]{0:T(128)S(1)} %add_rsqrt_fusion, bf16[]{:T(256)} %constant.128.clone.1), kind=kCustom, calls=%fused_computation.16 | custom fusion | flops 294912 | bytes 590338 | tf_op jit(solution)/shard_map/scatter | solution.py:34
  10.7 2.5 %all-to-all-done = bf16[4,64,1]{1,2,0:T(2,128)(2,1)S(1)} async-done(((bf16[4,64,1]{1,2,0:T(2,128)(2,1)}), bf16[4,64,1]{1,2,0:T(2,128)(2,1)S(1)}, u32[]{:S(2)}, u32[]{:S(2)}) %all-to-all-start) | async-done | bytes 544 | tf_op jit(solution)/shard_map/all_to_all | solution.py:43
  13.2 3.5 %all-to-all-start.2 = ((bf16[4,64,768]{2,1,0:T(8,128)(2,1)}), bf16[4,64,768]{2,1,0:T(8,128)(2,1)S(1)}, u32[]{:S(2)}, u32[]{:S(2)}) async-start(bf16[4,64,768]{2,1,0:T(8,128)(2,1)} %bitcast.3), calls=%async_computation.2 | async-start | bytes 786432 | tf_op jit(solution)/shard_map/all_to_all | solution.py:42
  16.8 0.6 reduce-window.6
  17.4 0.2 slice_reduce_fusion
  18.0 1.4 %scatter_custom_fusion.1 = f32[512]{0:T(512)S(1)} fusion(s32[256]{0:T(256)S(1)} %bitcast.34, f32[256]{0:T(256)S(1)} %reshape.237, f32[]{:T(128)} %constant.115.clone.1), kind=kCustom, calls=%fused_computation.54 | custom fusion | bytes 2052 | tf_op jit(solution)/shard_map/scatter | solution.py:71
  19.4 0.7 all_to_all.58
  20.0 2.4 %all-to-all-done.2 = bf16[4,64,768]{2,1,0:T(8,128)(2,1)S(1)} async-done(((bf16[4,64,768]{2,1,0:T(8,128)(2,1)}), bf16[4,64,768]{2,1,0:T(8,128)(2,1)S(1)}, u32[]{:S(2)}, u32[]{:S(2)}) %all-to-all-start.2) | async-done | bytes 393248 | tf_op jit(solution)/shard_map/all_to_all | solution.py:42
  22.5 4.9 %all-to-all-start.1 = ((bf16[8,64,1]{1,2,0:T(2,128)(2,1)}), bf16[8,64,1]{1,2,0:T(2,128)(2,1)S(1)}, u32[]{:S(2)}, u32[]{:S(2)}) async-start(bf16[8,64,1]{1,2,0:T(2,128)(2,1)} %all_to_all.58), calls=%async_computation.1 | async-start | bytes 8192 | tf_op jit(solution)/shard_map/all_to_all | solution.py:76
  27.4 2.6 %scatter_custom_fusion.3 = bf16[512,768]{1,0:T(8,128)(2,1)} fusion(s32[256]{0:T(256)S(1)} %bitcast.35, bf16[256,768]{1,0:T(8,128)(2,1)S(1)} %bitcast.29, bf16[]{:T(256)} %constant.128.clone.1), kind=kCustom, calls=%fused_computation.14 | custom fusion | bytes 786434 | tf_op jit(solution)/shard_map/scatter | solution.py:66
  29.9 3.0 %all-to-all-done.1 = bf16[8,64,1]{1,2,0:T(2,128)(2,1)S(1)} async-done(((bf16[8,64,1]{1,2,0:T(2,128)(2,1)}), bf16[8,64,1]{1,2,0:T(2,128)(2,1)S(1)}, u32[]{:S(2)}, u32[]{:S(2)}) %all-to-all-start.1) | async-done | bytes 1056 | tf_op jit(solution)/shard_map/all_to_all | solution.py:76
  32.9 3.5 %all-to-all-start.3 = ((bf16[8,64,768]{2,1,0:T(8,128)(2,1)}), bf16[8,64,768]{2,1,0:T(8,128)(2,1)S(1)}, u32[]{:S(2)}, u32[]{:S(2)}) async-start(bf16[8,64,768]{2,1,0:T(8,128)(2,1)} %bitcast.5), calls=%async_computation.3 | async-start | bytes 1572864 | tf_op jit(solution)/shard_map/all_to_all | solution.py:75
  36.6 20.7 %all-to-all-done.3 = bf16[8,64,768]{2,1,0:T(8,128)(2,1)S(1)} async-done(((bf16[8,64,768]{2,1,0:T(8,128)(2,1)}), bf16[8,64,768]{2,1,0:T(8,128)(2,1)S(1)}, u32[]{:S(2)}, u32[]{:S(2)}) %all-to-all-start.3) | async-done | bytes 786464 | tf_op jit(solution)/shard_map/all_to_all | solution.py:75
  57.4 0.7 fusion
  58.1 0.7 all_to_all.52
  58.7 3.3 %all-to-all-start.4 = ((f32[8,64,1]{1,2,0:T(1,128)}), f32[8,64,1]{1,2,0:T(1,128)S(1)}, u32[]{:S(2)}, u32[]{:S(2)}) async-start(f32[8,64,1]{1,2,0:T(1,128)} %bitcast.7), calls=%async_computation.4 | async-start | bytes 8192 | tf_op jit(solution)/shard_map/all_to_all | solution.py:103
  62.1 5.5 %all-to-all-done.4 = f32[8,64,1]{1,2,0:T(1,128)S(1)} async-done(((f32[8,64,1]{1,2,0:T(1,128)}), f32[8,64,1]{1,2,0:T(1,128)S(1)}, u32[]{:S(2)}, u32[]{:S(2)}) %all-to-all-start.4) | async-done | bytes 2080 | tf_op jit(solution)/shard_map/all_to_all | solution.py:103
  67.6 0.5 broadcast.365
  68.1 0.7 reduce.24
  68.8 1.9 %gather_fusion = f32[256]{0:T(256)S(1)} fusion(f32[512]{0:T(512)S(1)} %all_to_all.54, s32[1024]{0:T(1024)S(1)} %pad_clamp_fusion.1), kind=kCustom, calls=%fused_computation | custom fusion | bytes 3072 | tf_op jit(solution)/shard_map/gather | solution.py:104
  70.9 0.6 compare_select_fusion
  71.5 3.2 %all-to-all-start.5 = ((f32[4,64,1]{1,2,0:T(1,128)}), f32[4,64,1]{1,2,0:T(1,128)S(1)}, u32[]{:S(2)}, u32[]{:S(2)}) async-start(f32[4,64,1]{1,2,0:T(1,128)} %compare_select_fusion), calls=%async_computation.5 | async-start | bytes 4096 | tf_op jit(solution)/shard_map/all_to_all | solution.py:105
  74.7 4.5 %all-to-all-done.5 = f32[4,64,1]{1,2,0:T(1,128)S(1)} async-done(((f32[4,64,1]{1,2,0:T(1,128)}), f32[4,64,1]{1,2,0:T(1,128)S(1)}, u32[]{:S(2)}, u32[]{:S(2)}) %all-to-all-start.5) | async-done | bytes 1056 | tf_op jit(solution)/shard_map/all_to_all | solution.py:105
  79.2 0.7 reduce.25
  80.0 1.3 %gather_fusion.1 = f32[128]{0:T(128)S(1)} fusion(f32[256]{0:T(256)S(1)} %all_to_all.56, s32[1024]{0:T(1024)S(1)} %pad_clamp_fusion), kind=kCustom, calls=%fused_computation.1 | custom fusion | bytes 1536 | tf_op jit(solution)/shard_map/gather | solution.py:106
  81.4 0.4 copy-done.1
  81.8 38.2 %psum.7 = f32[128]{0:T(128)S(1)} all-reduce(f32[128]{0:T(128)S(1)} %maximum_reduce_fusion), channel_id=1, replica_groups=mesh['rows'=4,'cols'=8] {'rows','cols'}, use_global_device_ids=true, to_apply=%region_12.13 | all-reduce | flops 128 | bytes 1024 | tf_op jit(solution)/shard_map/psum | solution.py:110
  120.0 0.5 broadcast_multiply_fusion
  (34 shorter events, 1.6 us)
Async XLA Ops:
  0.6 8.0 %copy-start = (bf16[128,768]{1,0:T(8,128)(2,1)S(1)}, bf16[128,768]{1,0:T(8,128)(2,1)}, u32[]{:S(2)}) copy-start(bf16[128,768]{1,0:T(8,128)(2,1)} %param.2) | copy-start | bytes 589828
  3.5 9.7 %all-to-all-start = ((bf16[4,64,1]{1,2,0:T(2,128)(2,1)}), bf16[4,64,1]{1,2,0:T(2,128)(2,1)S(1)}, u32[]{:S(2)}, u32[]{:S(2)}) async-start(bf16[4,64,1]{1,2,0:T(2,128)(2,1)} %all_to_all.57), calls=%async_computation | async-start | bytes 4096 | tf_op jit(solution)/shard_map/all_to_all | solution.py:43
  13.2 9.3 %all-to-all-start.2 = ((bf16[4,64,768]{2,1,0:T(8,128)(2,1)}), bf16[4,64,768]{2,1,0:T(8,128)(2,1)S(1)}, u32[]{:S(2)}, u32[]{:S(2)}) async-start(bf16[4,64,768]{2,1,0:T(8,128)(2,1)} %bitcast.3), calls=%async_computation.2 | async-start | bytes 786432 | tf_op jit(solution)/shard_map/all_to_all | solution.py:42
  22.5 10.5 %all-to-all-start.1 = ((bf16[8,64,1]{1,2,0:T(2,128)(2,1)}), bf16[8,64,1]{1,2,0:T(2,128)(2,1)S(1)}, u32[]{:S(2)}, u32[]{:S(2)}) async-start(bf16[8,64,1]{1,2,0:T(2,128)(2,1)} %all_to_all.58), calls=%async_computation.1 | async-start | bytes 8192 | tf_op jit(solution)/shard_map/all_to_all | solution.py:76
  32.9 24.4 %all-to-all-start.3 = ((bf16[8,64,768]{2,1,0:T(8,128)(2,1)}), bf16[8,64,768]{2,1,0:T(8,128)(2,1)S(1)}, u32[]{:S(2)}, u32[]{:S(2)}) async-start(bf16[8,64,768]{2,1,0:T(8,128)(2,1)} %bitcast.5), calls=%async_computation.3 | async-start | bytes 1572864 | tf_op jit(solution)/shard_map/all_to_all | solution.py:75
  58.7 8.9 %all-to-all-start.4 = ((f32[8,64,1]{1,2,0:T(1,128)}), f32[8,64,1]{1,2,0:T(1,128)S(1)}, u32[]{:S(2)}, u32[]{:S(2)}) async-start(f32[8,64,1]{1,2,0:T(1,128)} %bitcast.7), calls=%async_computation.4 | async-start | bytes 8192 | tf_op jit(solution)/shard_map/all_to_all | solution.py:103
  71.5 7.7 %all-to-all-start.5 = ((f32[4,64,1]{1,2,0:T(1,128)}), f32[4,64,1]{1,2,0:T(1,128)S(1)}, u32[]{:S(2)}, u32[]{:S(2)}) async-start(f32[4,64,1]{1,2,0:T(1,128)} %compare_select_fusion), calls=%async_computation.5 | async-start | bytes 4096 | tf_op jit(solution)/shard_map/all_to_all | solution.py:105
  81.2 0.5 copy-start.1
where the time goes:
time: 121 us; the launch traced here: 120 us
  waiting for transfers between devices  38.6 us (32%)
  blocking collectives  38.2 us (32%)
  starting transfers between devices  23.7 us (20%)
  local copies, waits for them, and re-layouts  11.9 us (10%)
  other arithmetic  6.56 us (5%)
    psum x1, blocking collectives, shards(): bin_totals = lax.psum(jnp.sum(bin_weights, axis=0), ('rows', 'cols'))  38.2 us
    all_to_all x1, waiting for transfers between devices, shards(): lax.all_to_all(send_rows, 'cols', split_axis=0, concat_axis=0, tiled=True)  20.7 us
    all_to_all x1, waiting for transfers between devices, shards(): lax.all_to_all(best_owned, 'cols', split_axis=0, concat_axis=0, tiled=True)  5.5 us
    all_to_all x1, starting transfers between devices, shards(): lax.all_to_all(out_labels, 'rows', split_axis=0, concat_axis=0, tiled=True)  5.19 us
    all_to_all x1, starting transfers between devices, shards(): lax.all_to_all(send_labels, 'cols', split_axis=0, concat_axis=0, tiled=True)  4.88 us
    all_to_all x1, waiting for transfers between devices, shards(): lax.all_to_all(row_best, 'rows', split_axis=0, concat_axis=0, tiled=True)  4.48 us
    all_to_all x1, starting transfers between devices, shards(): lax.all_to_all(send_rows, 'cols', split_axis=0, concat_axis=0, tiled=True)  3.55 us
    all_to_all x1, starting transfers between devices, shards(): lax.all_to_all(outgoing, 'rows', split_axis=0, concat_axis=0, tiled=True)  3.46 us
  transfers between devices with their start and end apart: 6, of which 6 were waited for; matrix products, arithmetic and copies ran while one was open for 6% of the time, Pallas kernels for 0%

commit v1 on v0

--- a/solution.py
+++ b/solution.py
@@ -1,11 +1,16 @@
+import functools
+
 import jax
 import jax.numpy as jnp
 from jax import lax
+from jax.experimental import pallas as pl
+from jax.experimental.pallas import tpu as pltpu
 from jax.sharding import PartitionSpec as P
 
 CAP = 64
 GROUP_CLUSTERS = 16
 BINS = 128
+CORES = 2
 
 
 def from_partner(value, axis, bit):
@@ -111,8 +116,231 @@
     return (max_similarity, bin_totals / (doc_count * row_count * col_count))
 
 
+def plane_kernel(planes, doc_total, emb_ref, cluster_ref, best_ref, hist_ref, keys, send, queries, lab_send, labs,
+                 best_send, best_box, hist_send, hist_box, z_sems, hop_sems, core_sems, lab_sems, best_sems, hist_sems):
+    row = lax.axis_index("rows")
+    col = lax.axis_index("cols")
+    z, core = col // CORES, col % CORES
+    row_at = (row, row + 1 - 2 * (row % 2), row + 2 - 4 * (row // 2), 3 - row)
+    core_at = (core, 1 - core)
+    rows = len(row_at)
+
+    def device(m, k, d):
+        return (row_at[m], lax.rem(z + d, planes) * CORES + core_at[k])
+
+    peers = [(m, k, d) for d in range(planes) for k in range(CORES) for m in range(rows) if m or k or d]
+
+    def copy(source, target, sems, at, where):
+        return pltpu.make_async_remote_copy(
+            src_ref=source, dst_ref=target, send_sem=sems.at[(0, *at)], recv_sem=sems.at[(1, *at)],
+            device_id=where, device_id_type=pl.DeviceIdType.MESH)
+
+    barrier = pltpu.get_barrier_semaphore()
+    for peer in peers:
+        pl.semaphore_signal(barrier, inc=1, device_id=device(*peer), device_id_type=pl.DeviceIdType.MESH)
+
+    docs, width = emb_ref.shape
+    cluster = cluster_ref[...]
+    group = cluster // GROUP_CLUSTERS
+    local = (cluster - group * GROUP_CLUSTERS).astype(jnp.float32)
+    distance = group - z
+    distance = jnp.where(distance < 0, distance + planes, distance)
+    member = lax.broadcasted_iota(jnp.int32, (8, docs), 0) == distance
+    earlier = lax.broadcasted_iota(jnp.int32, (docs, docs), 0) < lax.broadcasted_iota(jnp.int32, (docs, docs), 1)
+    counts = jnp.dot(member.astype(jnp.bfloat16), earlier.astype(jnp.bfloat16), preferred_element_type=jnp.float32)
+    rank = jnp.sum(jnp.where(member, counts, 0.0), axis=0, keepdims=True).astype(jnp.int32)
+    place = distance * CAP + rank
+    onehot = (lax.broadcasted_iota(jnp.int32, (planes * CAP, docs), 0) == place).astype(jnp.bfloat16)
+    wide = lax.broadcasted_iota(jnp.int32, (128, docs), 0)
+    label_rows = jnp.where(member, local + 1.0, 0.0).astype(jnp.bfloat16)
+    label_slots = lax.dot_general(
+        label_rows, (wide == rank).astype(jnp.bfloat16), (((1,), (1,)), ((), ())), preferred_element_type=jnp.float32
+    ) - 1.0
+    values = emb_ref[...].astype(jnp.float32)
+    normed = (values * lax.rsqrt(jnp.sum(values * values, axis=1, keepdims=True) + 1e-06)).astype(jnp.bfloat16)
+    slots = jnp.dot(onehot, normed, preferred_element_type=jnp.float32).astype(jnp.bfloat16)
+    keys[0, 0] = slots[:CAP]
+    for d in range(planes):
+        lab_send[d] = label_slots[d : d + 1]
+        if d:
+            send[d - 1] = slots[d * CAP : (d + 1) * CAP]
+    labs[0, 0] = label_slots[0:1]
+
+    pl.semaphore_wait(barrier, len(peers))
+
+    here, there = (row, col), (row, z * CORES + core_at[1])
+    x_peer, y_peer = (row_at[1], col), (row_at[2], col)
+    half = CAP // 2
+    low, high = pl.ds(0, half), pl.ds(half, half)
+
+    def along_z(d):
+        return copy(send.at[d - 1], keys.at[d, 0], z_sems, (d,), device(0, 0, d))
+
+    def hop(n, d):
+        source, target, peer = (
+            (keys.at[d, 0], keys.at[d, 1], x_peer),
+            (keys.at[d, 0], keys.at[d, 2], y_peer),
+            (keys.at[d, 1, low], keys.at[d, 3, low], y_peer),
+            (keys.at[d, 2, high], keys.at[d, 3, high], x_peer),
+        )[n]
+        return copy(source, target, hop_sems, (n, d), peer)
+
+    def across(m, d):
+        return copy(keys.at[d, m], keys.at[d, rows + m], core_sems, (m, d), there)
+
+    def label_copy(m, k, d):
+        return copy(lab_send.at[d], labs.at[d, k * rows + m], lab_sems, (d, k * rows + m), device(m, k, d))
+
+    def best_copy(d):
+        return copy(best_send.at[d // 2], best_box.at[d], best_sems, (d,), (row, lax.rem(z + planes - d, planes) * CORES + core))
+
+    def hist_copy(m, k, d):
+        return copy(hist_send, hist_box.at[d, k * rows + m], hist_sems, (d, k * rows + m), device(m, k, d))
+
+    def own(d):
+        if d:
+            along_z(d).wait_recv()
+        hop(0, d).start()
+        hop(1, d).start()
+        across(0, d).start()
+
+    def forward(d):
+        hop(0, d).wait_recv()
+        hop(2, d).start()
+        across(1, d).start()
+        hop(1, d).wait_recv()
+        hop(3, d).start()
+        across(2, d).start()
+
+    def corner(d):
+        hop(2, d).wait_recv()
+        hop(3, d).wait_recv()
+        across(3, d).start()
+
+    for d in range(1, planes):
+        along_z(d).start()
+    own(0)
+    for peer in peers:
+        label_copy(*peer).start()
+    for d in range(1, planes):
+        own(d)
+        forward(d - 1)
+    for peer in peers:
+        label_copy(*peer).wait_recv()
+    corner(0)
+    for d in range(planes):
+        queries[d * CAP : (d + 1) * CAP, :] = keys[d, 0]
+    corner(1)
+    lanes = lax.broadcasted_iota(jnp.int32, (CORES * rows, 128), 1)
+    tables = [labs[d, :, 0, :] for d in range(planes)]
+    query_labels = jnp.concatenate(
+        [jnp.where(lanes < CAP, tables[d], pltpu.roll(tables[d + 1], CAP, 1))[0:1] for d in range(0, planes, 2)], axis=1
+    )
+    query_count = planes * CAP
+    key_index = lax.broadcasted_iota(jnp.int32, (CAP, query_count), 0)
+    query_index = lax.broadcasted_iota(jnp.int32, (CAP, query_count), 1)
+    best = jnp.full((8, query_count), -1.0, jnp.float32)
+    for d in range(planes):
+        if d == planes - 2:
+            forward(planes - 1)
+        if d >= planes - 2:
+            corner(d)
+        for m in range(rows):
+            across(m, d).wait_recv()
+        block = keys[d].reshape(CORES * rows * CAP, width)
+        scores = lax.dot_general(block, queries[...], (((1,), (1,)), ((), ())), preferred_element_type=jnp.float32)
+        key_labels = tables[d].T
+        for j in range(CORES * rows):
+            same = (key_labels[:CAP, j : j + 1] == query_labels) & (query_labels >= 0.0)
+            if j == 0:
+                same = same & (key_index + d * CAP != query_index)
+            part = jnp.where(same, scores[j * CAP : (j + 1) * CAP], -1.0)
+            best = jnp.maximum(best, jnp.max(part.reshape(CAP // 8, 8, query_count), axis=0))
+    best = jnp.max(best, axis=0, keepdims=True)
+    for n in range(planes // 2):
+        best_send[n] = best[:, n * 128 : (n + 1) * 128]
+    best_box[0] = best[:, :128]
+    for d in range(1, planes):
+        best_copy(d).start()
+
+    bin_width = 2.0 / (BINS - 1)
+    centers = -1.0 + lax.broadcasted_iota(jnp.int32, (BINS, query_count), 0).astype(jnp.float32) * bin_width
+    weights = jnp.maximum(1.0 - jnp.abs(best - centers) / bin_width, 0.0)
+    filled = jnp.broadcast_to((query_labels >= 0.0).astype(jnp.float32), (8, query_count))
+    totals = lax.dot_general(
+        filled, weights, (((1,), (1,)), ((), ())), precision=lax.Precision.HIGHEST, preferred_element_type=jnp.float32
+    )[0:1]
+    hist_send[...] = totals
+    hist_box[0, 0] = totals
+    for peer in peers:
+        hist_copy(*peer).start()
+
+    for d in range(1, planes):
+        best_copy(d).wait_recv()
+    answers = jnp.concatenate([best_box[d] for d in range(planes)] * (8 // planes), axis=0)
+    found = [
+        jnp.dot(answers, (wide == rank + n * CAP).astype(jnp.float32), precision=lax.Precision.HIGHEST,
+                preferred_element_type=jnp.float32)
+        for n in range(2)
+    ]
+    odd = lax.broadcasted_iota(jnp.int32, (8, docs), 0) % 2 == 1
+    best_ref[...] = jnp.sum(jnp.where(member, jnp.where(odd, found[1], found[0]), 0.0), axis=0, keepdims=True)
+
+    for d in range(1, planes):
+        along_z(d).wait_send()
+        best_copy(d).wait_send()
+    for d in range(planes):
+        for n in range(4):
+            hop(n, d).wait_send()
+        for m in range(rows):
+            across(m, d).wait_send()
+    for peer in peers:
+        label_copy(*peer).wait_send()
+    for peer in peers:
+        hist_copy(*peer).wait()
+    hist_ref[...] = jnp.sum(jnp.sum(hist_box[...], axis=0), axis=0) / doc_total
+
+
+def plane_shards(embeddings, document_cluster_index):
+    rows, cols = lax.axis_size("rows"), lax.axis_size("cols")
+    planes = cols // CORES
+    docs, width = embeddings.shape
+    blocks = CORES * rows
+    vmem = pl.BlockSpec(memory_space=pltpu.VMEM)
+    dma = pltpu.SemaphoreType.DMA
+    row = lambda *lead: pltpu.VMEM((*lead, 1, 128), jnp.float32)
+    best, histogram = pl.pallas_call(
+        functools.partial(plane_kernel, planes, docs * rows * cols),
+        out_shape=(jax.ShapeDtypeStruct((1, docs), jnp.float32), jax.ShapeDtypeStruct((1, BINS), jnp.float32)),
+        in_specs=[vmem, vmem],
+        out_specs=(vmem, vmem),
+        scratch_shapes=[
+            pltpu.VMEM((planes, blocks, CAP, width), jnp.bfloat16),
+            pltpu.VMEM((planes - 1, CAP, width), jnp.bfloat16),
+            pltpu.VMEM((planes * CAP, width), jnp.bfloat16),
+            row(planes),
+            row(planes, blocks),
+            row(planes // 2),
+            row(planes),
+            row(),
+            row(planes, blocks),
+            dma((2, planes)),
+            dma((2, 4, planes)),
+            dma((2, rows, planes)),
+            dma((2, planes, blocks)),
+            dma((2, planes)),
+            dma((2, planes, blocks)),
+        ],
+        compiler_params=pltpu.CompilerParams(collective_id=0, has_side_effects=True),
+    )(embeddings, document_cluster_index.reshape(1, docs))
+    return best.reshape(docs), histogram.reshape(BINS)
+
+
 def solution(mesh):
     placed = (P(("rows", "cols"), None), P(("rows", "cols")))
+    rows, planes = mesh.shape["rows"], mesh.shape["cols"] // CORES
+    direct = rows == 4 and planes == rows
     return jax.shard_map(
-        shards, mesh=mesh, in_specs=placed, out_specs=(P(("rows", "cols")), P()), check_vma=False
-    )
+        plane_shards if direct else shards, mesh=mesh, in_specs=placed,
+        out_specs=(P(("rows", "cols")), P()), check_vma=False
+    )

time: 121 us -> 40.3 us (0.33)
  waiting for transfers between devices: 38.6 us -> 0 us
  blocking collectives: 38.2 us -> 0 us
  Pallas kernels: 0 us -> 37.7 us
  starting transfers between devices: 23.7 us -> 0 us
  local copies, waits for them, and re-layouts: 11.9 us -> 1.8 us
  other arithmetic: 6.56 us -> 0 us
    all_to_all x6 -> x0, waiting for transfers between devices: 38.6 us -> none  [the longest x1 20.7 us: shards(): lax.all_to_all(send_rows, 'cols', split_axis=0, concat_axis=0, tiled=True)]
    psum x1 -> x0, blocking collectives: 38.2 us -> none  [shards(): bin_totals = lax.psum(jnp.sum(bin_weights, axis=0), ('rows', 'cols'))]
    pallas_call x0 -> x1, Pallas kernels: none -> 37.7 us  [plane_shards(): pl.pallas_call(functools.partial(plane_kernel, planes, docs * rows * cols...]
    all_to_all x6 -> x0, starting transfers between devices: 23.7 us -> none  [the longest x1 5.19 us: shards(): lax.all_to_all(out_labels, 'rows', split_axis=0, concat_axis=0, tiled=True)]
    scatter x3 -> x0, local copies, waits for them, and re-layouts: 4.95 us -> none  [the longest x1 2.57 us: shards(): jnp.zeros((send_total, width), jnp.bfloat16).at[send_place]]
    gather x3 -> x0, local copies, waits for them, and re-layouts: 3.29 us -> none  [the longest x2 2.03 us: shards(): came_back[jnp.minimum(send_place, send_total - 1)]]
    all_to_all x6 -> x0, local copies, waits for them, and re-layouts: 2.67 us -> none  [the longest x3 1.26 us: shards(): lax.all_to_all(best_owned, 'cols', split_axis=0, concat_axis=0, tiled=True)]
    scatter x1 -> x0, other arithmetic: 1.93 us -> none  [shards(): jnp.zeros((slot_count, width), jnp.bfloat16).at[places].set(normed)]
  transfers between devices with their start and end apart: 6 -> 0, of which waited for: 6 -> 0; matrix products, arithmetic and copies ran while one was open for 6% -> 0% of each run, Pallas kernels for 0% -> 0%
where the time goes in v1:
time: 40.3 us; the launch traced here: 40.2 us
  Pallas kernels  37.7 us (94%)
  local copies, waits for them, and re-layouts  1.8 us (4%)
  between operations  0.65 us (2%)
    pallas_call x1, Pallas kernels, plane_shards(): pl.pallas_call(functools.partial(plane_kernel, planes, docs * rows * cols...  37.7 us
    unnamed x6, local copies, waits for them, and re-layouts  1.8 us

profile of v1, /device:TPU:0, one launch (start us, length us, event | category | flops | bytes accessed | tf_op | source)
XLA Modules:
  0.0 40.2 jit_solution(10824999669385096128)
XLA Ops:
  0.6 37.7 %shard_map.41 = (f32[1,128]{1,0:T(1,128)}, f32[1,128]{1,0:T(1,128)}) custom-call(bf16[128,768]{1,0:T(8,128)(2,1)} %emb_ref.1, s32[1,128]{1,0:T(1,128)} %bitcast.3), custom_call_target="tpu_custom_call" | custom-call | tf_op jit(solution)/shard_map/pallas_call | solution.py:312
  38.3 0.0 copy-start.1
  38.4 0.7 %copy-done.1 = f32[1,128]{1,0:T(1,128)S(1)} copy-done((f32[1,128]{1,0:T(1,128)S(1)}, f32[1,128]{1,0:T(1,128)}, u32[]{:S(2)}) %copy-start.1) | copy-done | bytes 536
  39.0 0.0 copy-start
  39.0 0.5 %copy.6 = f32[128]{0:T(128)} copy(f32[128]{0:T(128)S(1)} %bitcast.5) | data formatting | bytes 1024
  39.5 0.1 copy-done
  39.6 0.5 %copy.7 = f32[128]{0:T(128)} copy(f32[128]{0:T(128)S(1)} %bitcast.4) | data formatting | bytes 1024
Async XLA Ops:
  38.3 0.7 %copy-start.1 = (f32[1,128]{1,0:T(1,128)S(1)}, f32[1,128]{1,0:T(1,128)}, u32[]{:S(2)}) copy-start(f32[1,128]{1,0:T(1,128)} %get-tuple-element.4) | copy-start | bytes 1540
  39.0 0.6 %copy-start = (f32[1,128]{1,0:T(1,128)S(1)}, f32[1,128]{1,0:T(1,128)}, u32[]{:S(2)}) copy-start(f32[1,128]{1,0:T(1,128)} %get-tuple-element.5) | copy-start | bytes 1540

commit v2 on v1

--- a/solution.py
+++ b/solution.py
@@ -116,8 +116,9 @@
     return (max_similarity, bin_totals / (doc_count * row_count * col_count))
 
 
-def plane_kernel(planes, doc_total, emb_ref, cluster_ref, best_ref, hist_ref, keys, send, queries, lab_send, labs,
-                 best_send, best_box, hist_send, hist_box, z_sems, hop_sems, core_sems, lab_sems, best_sems, hist_sems):
+def plane_kernel(planes, doc_total, emb_hbm, cluster_hbm, best_ref, hist_ref, emb_ref, cluster_ref, keys, send, queries,
+                 lab_send, labs, best_send, best_box, hist_send, hist_box, in_sems, z_sems, hop_sems, core_sems, best_sems,
+                 hist_sems):
     row = lax.axis_index("rows")
     col = lax.axis_index("cols")
     z, core = col // CORES, col % CORES
@@ -136,8 +137,14 @@
             device_id=where, device_id_type=pl.DeviceIdType.MESH)
 
     barrier = pltpu.get_barrier_semaphore()
-    for peer in peers:
+    greeted = [(0, 0, d) for d in range(1, planes)] + [(1, 0, 0), (2, 0, 0), (0, 1, 0)]
+    for peer in greeted:
         pl.semaphore_signal(barrier, inc=1, device_id=device(*peer), device_id_type=pl.DeviceIdType.MESH)
+    loads = [pltpu.make_async_copy(emb_hbm, emb_ref, in_sems.at[0]), pltpu.make_async_copy(cluster_hbm, cluster_ref, in_sems.at[1])]
+    for load in loads:
+        load.start()
+    for load in loads:
+        load.wait()
 
     docs, width = emb_ref.shape
     cluster = cluster_ref[...]
@@ -160,81 +167,115 @@
     normed = (values * lax.rsqrt(jnp.sum(values * values, axis=1, keepdims=True) + 1e-06)).astype(jnp.bfloat16)
     slots = jnp.dot(onehot, normed, preferred_element_type=jnp.float32).astype(jnp.bfloat16)
     keys[0, 0] = slots[:CAP]
-    for d in range(planes):
-        lab_send[d] = label_slots[d : d + 1]
-        if d:
-            send[d - 1] = slots[d * CAP : (d + 1) * CAP]
+    for d in range(1, planes):
+        lab_send[d - 1] = label_slots[d : d + 1]
+        send[d - 1] = slots[d * CAP : (d + 1) * CAP]
     labs[0, 0] = label_slots[0:1]
 
-    pl.semaphore_wait(barrier, len(peers))
+    pl.semaphore_wait(barrier, len(greeted))
 
     here, there = (row, col), (row, z * CORES + core_at[1])
     x_peer, y_peer = (row_at[1], col), (row_at[2], col)
     half = CAP // 2
     low, high = pl.ds(0, half), pl.ds(half, half)
 
+    def slot(d, plane):
+        return d if d == 0 else planes - d + (plane % 2) * (2 * d - planes)
+
     def along_z(d):
-        return copy(send.at[d - 1], keys.at[d, 0], z_sems, (d,), device(0, 0, d))
-
-    def hop(n, d):
-        source, target, peer = (
-            (keys.at[d, 0], keys.at[d, 1], x_peer),
-            (keys.at[d, 0], keys.at[d, 2], y_peer),
-            (keys.at[d, 1, low], keys.at[d, 3, low], y_peer),
-            (keys.at[d, 2, high], keys.at[d, 3, high], x_peer),
-        )[n]
-        return copy(source, target, hop_sems, (n, d), peer)
-
-    def across(m, d):
-        return copy(keys.at[d, m], keys.at[d, rows + m], core_sems, (m, d), there)
-
-    def label_copy(m, k, d):
-        return copy(lab_send.at[d], labs.at[d, k * rows + m], lab_sems, (d, k * rows + m), device(m, k, d))
-
-    def best_copy(d):
-        return copy(best_send.at[d // 2], best_box.at[d], best_sems, (d,), (row, lax.rem(z + planes - d, planes) * CORES + core))
+        s = slot(d, lax.rem(z + d, planes))
+        return [
+            copy(lab_send.at[d - 1], labs.at[s, 0], z_sems, (1, s), device(0, 0, d)),
+            copy(send.at[d - 1], keys.at[s, 0], z_sems, (0, s), device(0, 0, d)),
+        ]
+
+    def from_z(s):
+        return [
+            copy(lab_send.at[0], labs.at[s, 0], z_sems, (1, s), device(0, 0, 1)),
+            copy(send.at[0], keys.at[s, 0], z_sems, (0, s), device(0, 0, 1)),
+        ]
+
+    def hop(n, s):
+        if n < 2:
+            peer = (x_peer, y_peer)[n]
+            return [
+                copy(labs.at[s, 0], labs.at[s, n + 1], hop_sems, (n, 1, s), peer),
+                copy(keys.at[s, 0], keys.at[s, n + 1], hop_sems, (n, 0, s), peer),
+            ]
+        if n == 2:
+            return [
+                copy(labs.at[s, 1], labs.at[s, 3], hop_sems, (n, 1, s), y_peer),
+                copy(keys.at[s, 1, low], keys.at[s, 3, low], hop_sems, (n, 0, s), y_peer),
+            ]
+        return [copy(keys.at[s, 2, high], keys.at[s, 3, high], hop_sems, (n, 0, s), x_peer)]
+
+    def across(m, s):
+        return [
+            copy(labs.at[s, m], labs.at[s, rows + m], core_sems, (m, 1, s), there),
+            copy(keys.at[s, m], keys.at[s, rows + m], core_sems, (m, 0, s), there),
+        ]
+
+    def start(copies):
+        for item in copies:
+            item.start()
+
+    def wait_recv(copies):
+        for item in copies:
+            item.wait_recv()
+
+    def wait_send(copies):
+        for item in copies:
+            item.wait_send()
+
+    def best_copy(s):
+        d = slot(s, z)
+        return copy(best_send.at[s // 2], best_box.at[d], best_sems, (d,), (row, lax.rem(z + planes - d, planes) * CORES + core))
 
     def hist_copy(m, k, d):
         return copy(hist_send, hist_box.at[d, k * rows + m], hist_sems, (d, k * rows + m), device(m, k, d))
 
-    def own(d):
-        if d:
-            along_z(d).wait_recv()
-        hop(0, d).start()
-        hop(1, d).start()
-        across(0, d).start()
-
-    def forward(d):
-        hop(0, d).wait_recv()
-        hop(2, d).start()
-        across(1, d).start()
-        hop(1, d).wait_recv()
-        hop(3, d).start()
-        across(2, d).start()
-
-    def corner(d):
-        hop(2, d).wait_recv()
-        hop(3, d).wait_recv()
-        across(3, d).start()
-
-    for d in range(1, planes):
-        along_z(d).start()
+    def own(s):
+        if s:
+            wait_recv(from_z(s))
+        start(hop(0, s))
+        start(hop(1, s))
+        start(across(0, s))
+
+    def forward(s):
+        wait_recv(hop(0, s))
+        start(hop(2, s))
+        start(across(1, s))
+        wait_recv(hop(1, s))
+        start(hop(3, s))
+        start(across(2, s))
+
+    def corner(s):
+        wait_recv(hop(2, s))
+        wait_recv(hop(3, s))
+        start(across(3, s))
+
+    @pl.when(z < planes // 2)
+    def _():
+        for d in range(planes - 1, 0, -1):
+            start(along_z(d))
+
+    @pl.when(z >= planes // 2)
+    def _():
+        for d in range(1, planes):
+            start(along_z(d))
+
     own(0)
-    for peer in peers:
-        label_copy(*peer).start()
-    for d in range(1, planes):
-        own(d)
-        forward(d - 1)
-    for peer in peers:
-        label_copy(*peer).wait_recv()
+    for s in range(1, planes):
+        own(s)
+        forward(s - 1)
     corner(0)
-    for d in range(planes):
-        queries[d * CAP : (d + 1) * CAP, :] = keys[d, 0]
+    for s in range(planes):
+        queries[s * CAP : (s + 1) * CAP, :] = keys[s, 0]
     corner(1)
-    lanes = lax.broadcasted_iota(jnp.int32, (CORES * rows, 128), 1)
-    tables = [labs[d, :, 0, :] for d in range(planes)]
+    lanes = lax.broadcasted_iota(jnp.int32, (1, 128), 1)
+    query_tables = [labs[s, 0] for s in range(planes)]
     query_labels = jnp.concatenate(
-        [jnp.where(lanes < CAP, tables[d], pltpu.roll(tables[d + 1], CAP, 1))[0:1] for d in range(0, planes, 2)], axis=1
+        [jnp.where(lanes < CAP, query_tables[s], pltpu.roll(query_tables[s + 1], CAP, 1)) for s in range(0, planes, 2)], axis=1
     )
     query_count = planes * CAP
     key_index = lax.broadcasted_iota(jnp.int32, (CAP, query_count), 0)
@@ -246,10 +287,10 @@
         if d >= planes - 2:
             corner(d)
         for m in range(rows):
-            across(m, d).wait_recv()
+            wait_recv(across(m, d))
         block = keys[d].reshape(CORES * rows * CAP, width)
         scores = lax.dot_general(block, queries[...], (((1,), (1,)), ((), ())), preferred_element_type=jnp.float32)
-        key_labels = tables[d].T
+        key_labels = labs[d, :, 0, :].T
         for j in range(CORES * rows):
             same = (key_labels[:CAP, j : j + 1] == query_labels) & (query_labels >= 0.0)
             if j == 0:
@@ -272,7 +313,7 @@
     )[0:1]
     hist_send[...] = totals
     hist_box[0, 0] = totals
-    for peer in peers:
+    for peer in sorted(peers, key=lambda p: -((p[0] > 0) + (p[0] == 3) + (p[2] > 0))):
         hist_copy(*peer).start()
 
     for d in range(1, planes):
@@ -287,15 +328,13 @@
     best_ref[...] = jnp.sum(jnp.where(member, jnp.where(odd, found[1], found[0]), 0.0), axis=0, keepdims=True)
 
     for d in range(1, planes):
-        along_z(d).wait_send()
+        wait_send(along_z(d))
         best_copy(d).wait_send()
-    for d in range(planes):
+    for s in range(planes):
         for n in range(4):
-            hop(n, d).wait_send()
+            wait_send(hop(n, s))
         for m in range(rows):
-            across(m, d).wait_send()
-    for peer in peers:
-        label_copy(*peer).wait_send()
+            wait_send(across(m, s))
     for peer in peers:
         hist_copy(*peer).wait()
     hist_ref[...] = jnp.sum(jnp.sum(hist_box[...], axis=0), axis=0) / doc_total
@@ -306,28 +345,30 @@
     planes = cols // CORES
     docs, width = embeddings.shape
     blocks = CORES * rows
-    vmem = pl.BlockSpec(memory_space=pltpu.VMEM)
+    hbm, vmem = pl.BlockSpec(memory_space=pl.ANY), pl.BlockSpec(memory_space=pltpu.VMEM)
     dma = pltpu.SemaphoreType.DMA
     row = lambda *lead: pltpu.VMEM((*lead, 1, 128), jnp.float32)
     best, histogram = pl.pallas_call(
         functools.partial(plane_kernel, planes, docs * rows * cols),
-        out_shape=(jax.ShapeDtypeStruct((1, docs), jnp.float32), jax.ShapeDtypeStruct((1, BINS), jnp.float32)),
-        in_specs=[vmem, vmem],
+        out_shape=(pltpu.VMEM((1, docs), jnp.float32), pltpu.VMEM((1, BINS), jnp.float32)),
+        in_specs=[hbm, hbm],
         out_specs=(vmem, vmem),
         scratch_shapes=[
+            pltpu.VMEM((docs, width), jnp.bfloat16),
+            pltpu.VMEM((1, docs), jnp.int32),
             pltpu.VMEM((planes, blocks, CAP, width), jnp.bfloat16),
             pltpu.VMEM((planes - 1, CAP, width), jnp.bfloat16),
             pltpu.VMEM((planes * CAP, width), jnp.bfloat16),
-            row(planes),
+            row(planes - 1),
             row(planes, blocks),
             row(planes // 2),
             row(planes),
             row(),
             row(planes, blocks),
-            dma((2, planes)),
-            dma((2, 4, planes)),
-            dma((2, rows, planes)),
-            dma((2, planes, blocks)),
+            dma((2,)),
+            dma((2, 2, planes)),
+            dma((2, 4, 2, planes)),
+            dma((2, rows, 2, planes)),
             dma((2, planes)),
             dma((2, planes, blocks)),
         ],

time: 40.3 us -> 36.9 us (0.916)
  Pallas kernels: 37.7 us -> 35.1 us
  local copies, waits for them, and re-layouts: 1.8 us -> 1.02 us
    pallas_call x1, Pallas kernels: 37.7 us -> 35.1 us  [plane_shards(): pl.pallas_call(functools.partial(plane_kernel, planes, docs * rows * cols...]
    unnamed x6 -> x2, local copies, waits for them, and re-layouts: 1.8 us -> 1.02 us
where the time goes in v2:
time: 36.9 us; the launch traced here: 36.8 us
  Pallas kernels  35.1 us (95%)
  local copies, waits for them, and re-layouts  1.02 us (3%)
  between operations  0.64 us (2%)
    pallas_call x1, Pallas kernels, plane_shards(): pl.pallas_call(functools.partial(plane_kernel, planes, docs * rows * cols...  35.1 us
    unnamed x2, local copies, waits for them, and re-layouts  1.02 us

profile of v2, /device:TPU:0, one launch (start us, length us, event | category | flops | bytes accessed | tf_op | source)
XLA Modules:
  0.0 36.8 jit_solution(4340686807341195261)
XLA Ops:
  0.6 35.1 %shard_map.41 = (f32[1,128]{1,0:T(1,128)S(1)}, f32[1,128]{1,0:T(1,128)S(1)}) custom-call(bf16[128,768]{1,0:T(8,128)(2,1)} %emb_hbm.1, s32[1,128]{1,0:T(1,128)} %bitcast.5), custom_call_target="tpu_custom_call" | custom-call | tf_op jit(solution)/shard_map/pallas_call | solution.py:351
  35.8 0.5 %copy.6 = f32[128]{0:T(128)} copy(f32[128]{0:T(128)S(1)} %bitcast.4) | data formatting | bytes 1024
  36.3 0.5 %copy.7 = f32[128]{0:T(128)} copy(f32[128]{0:T(128)S(1)} %bitcast.3) | data formatting | bytes 1024

commit v3 on v2

--- a/solution.py
+++ b/solution.py
@@ -117,7 +117,7 @@
 
 
 def plane_kernel(planes, doc_total, emb_hbm, cluster_hbm, best_ref, hist_ref, emb_ref, cluster_ref, keys, send, queries,
-                 lab_send, labs, best_send, best_box, hist_send, hist_box, in_sems, z_sems, hop_sems, core_sems, best_sems,
+                 lab_send, labs, cross_send, cross_box, best_send, best_box, hist_send, hist_box, in_sems, z_sems, hop_sems, core_sems, cross_sems, best_sems,
                  hist_sems):
     row = lax.axis_index("rows")
     col = lax.axis_index("cols")
@@ -125,6 +125,7 @@
     row_at = (row, row + 1 - 2 * (row % 2), row + 2 - 4 * (row // 2), 3 - row)
     core_at = (core, 1 - core)
     rows = len(row_at)
+    near = rows - 1
 
     def device(m, k, d):
         return (row_at[m], lax.rem(z + d, planes) * CORES + core_at[k])
@@ -171,6 +172,9 @@
         lab_send[d - 1] = label_slots[d : d + 1]
         send[d - 1] = slots[d * CAP : (d + 1) * CAP]
     labs[0, 0] = label_slots[0:1]
+    for s in range(planes):
+        for j in range(CORES * near, 8):
+            labs[s, j] = jnp.full((1, 128), -1.0, jnp.float32)
 
     pl.semaphore_wait(barrier, len(greeted))
 
@@ -182,37 +186,35 @@
     def slot(d, plane):
         return d if d == 0 else planes - d + (plane % 2) * (2 * d - planes)
 
+    def z_copies(source, target, where):
+        return [
+            copy(lab_send.at[source], labs.at[target, 0], z_sems, (2, target), where),
+            copy(send.at[source, low], keys.at[target, 0, low], z_sems, (0, target), where),
+            copy(send.at[source, high], keys.at[target, 0, high], z_sems, (1, target), where),
+        ]
+
     def along_z(d):
-        s = slot(d, lax.rem(z + d, planes))
-        return [
-            copy(lab_send.at[d - 1], labs.at[s, 0], z_sems, (1, s), device(0, 0, d)),
-            copy(send.at[d - 1], keys.at[s, 0], z_sems, (0, s), device(0, 0, d)),
-        ]
+        return z_copies(d - 1, slot(d, lax.rem(z + d, planes)), device(0, 0, d))
 
     def from_z(s):
-        return [
-            copy(lab_send.at[0], labs.at[s, 0], z_sems, (1, s), device(0, 0, 1)),
-            copy(send.at[0], keys.at[s, 0], z_sems, (0, s), device(0, 0, 1)),
-        ]
+        return z_copies(0, s, device(0, 0, 1))
 
     def hop(n, s):
-        if n < 2:
-            peer = (x_peer, y_peer)[n]
-            return [
-                copy(labs.at[s, 0], labs.at[s, n + 1], hop_sems, (n, 1, s), peer),
-                copy(keys.at[s, 0], keys.at[s, n + 1], hop_sems, (n, 0, s), peer),
-            ]
-        if n == 2:
-            return [
-                copy(labs.at[s, 1], labs.at[s, 3], hop_sems, (n, 1, s), y_peer),
-                copy(keys.at[s, 1, low], keys.at[s, 3, low], hop_sems, (n, 0, s), y_peer),
-            ]
-        return [copy(keys.at[s, 2, high], keys.at[s, 3, high], hop_sems, (n, 0, s), x_peer)]
+        source, target, part, peer = (
+            (0, 1, low, x_peer),
+            (0, 1, high, x_peer),
+            (0, 2, high, y_peer),
+            (0, 2, low, y_peer),
+        )[n]
+        rest = [copy(keys.at[s, source, part], keys.at[s, target, part], hop_sems, (n, 0, s), peer)]
+        if n % 2 == 0:
+            rest = [copy(labs.at[s, source], labs.at[s, target], hop_sems, (n, 1, s), peer)] + rest
+        return rest
 
     def across(m, s):
         return [
-            copy(labs.at[s, m], labs.at[s, rows + m], core_sems, (m, 1, s), there),
-            copy(keys.at[s, m], keys.at[s, rows + m], core_sems, (m, 0, s), there),
+            copy(labs.at[s, m], labs.at[s, near + m], core_sems, (m, 1, s), there),
+            copy(keys.at[s, m], keys.at[s, near + m], core_sems, (m, 0, s), there),
         ]
 
     def start(copies):
@@ -235,24 +237,26 @@
         return copy(hist_send, hist_box.at[d, k * rows + m], hist_sems, (d, k * rows + m), device(m, k, d))
 
     def own(s):
+        first, second = [], []
         if s:
-            wait_recv(from_z(s))
+            came = from_z(s)
+            first, second = came[:2], came[2:]
+        wait_recv(first)
         start(hop(0, s))
+        start(hop(3, s))
+        wait_recv(second)
+        start(hop(2, s))
         start(hop(1, s))
         start(across(0, s))
 
     def forward(s):
-        wait_recv(hop(0, s))
-        start(hop(2, s))
+        wait_recv(hop(0, s) + hop(1, s))
         start(across(1, s))
-        wait_recv(hop(1, s))
-        start(hop(3, s))
+        wait_recv(hop(2, s) + hop(3, s))
         start(across(2, s))
 
-    def corner(s):
-        wait_recv(hop(2, s))
-        wait_recv(hop(3, s))
-        start(across(3, s))
+    def cross_copy(n):
+        return copy(cross_send.at[n], cross_box.at[n], cross_sems, (n,), (x_peer, y_peer)[n])
 
     @pl.when(z < planes // 2)
     def _():
@@ -268,36 +272,70 @@
     for s in range(1, planes):
         own(s)
         forward(s - 1)
-    corner(0)
-    for s in range(planes):
-        queries[s * CAP : (s + 1) * CAP, :] = keys[s, 0]
-    corner(1)
+    last = planes - 1
+    query_count = planes * CAP
     lanes = lax.broadcasted_iota(jnp.int32, (1, 128), 1)
-    query_tables = [labs[s, 0] for s in range(planes)]
-    query_labels = jnp.concatenate(
-        [jnp.where(lanes < CAP, query_tables[s], pltpu.roll(query_tables[s + 1], CAP, 1)) for s in range(0, planes, 2)], axis=1
-    )
-    query_count = planes * CAP
     key_index = lax.broadcasted_iota(jnp.int32, (CAP, query_count), 0)
     query_index = lax.broadcasted_iota(jnp.int32, (CAP, query_count), 1)
-    best = jnp.full((8, query_count), -1.0, jnp.float32)
-    for d in range(planes):
-        if d == planes - 2:
-            forward(planes - 1)
-        if d >= planes - 2:
-            corner(d)
-        for m in range(rows):
-            wait_recv(across(m, d))
-        block = keys[d].reshape(CORES * rows * CAP, width)
-        scores = lax.dot_general(block, queries[...], (((1,), (1,)), ((), ())), preferred_element_type=jnp.float32)
-        key_labels = labs[d, :, 0, :].T
-        for j in range(CORES * rows):
-            same = (key_labels[:CAP, j : j + 1] == query_labels) & (query_labels >= 0.0)
-            if j == 0:
-                same = same & (key_index + d * CAP != query_index)
-            part = jnp.where(same, scores[j * CAP : (j + 1) * CAP], -1.0)
+
+    def collect(n, j, s):
+        queries[n, s * CAP : (s + 1) * CAP, :] = keys[s, j]
+
+    def labels_of(j):
+        pieces = [labs[s, j] for s in range(planes)]
+        return jnp.concatenate(
+            [jnp.where(lanes < CAP, pieces[s], pltpu.roll(pieces[s + 1], CAP, 1)) for s in range(0, planes, 2)], axis=1
+        )
+
+    def compare(best, block, key_labels, query, query_labels, skip):
+        scores = lax.dot_general(block, query, (((1,), (1,)), ((), ())), preferred_element_type=jnp.float32)
+        for i, column in enumerate(key_labels):
+            same = (column == query_labels) & (query_labels >= 0.0)
+            if i == 0 and skip is not None:
+                same = same & (key_index + skip * CAP != query_index)
+            part = jnp.where(same, scores[i * CAP : (i + 1) * CAP], -1.0)
             best = jnp.maximum(best, jnp.max(part.reshape(CAP // 8, 8, query_count), axis=0))
+        return best
+
+    def own_group(best, s, query_labels):
+        block = keys[s].reshape(CORES * near * CAP, width)
+        table = labs[s, :, 0, :].T
+        columns = [table[:CAP, j : j + 1] for j in range(CORES * near)]
+        return compare(best, block, columns, queries[0], query_labels, s)
+
+    for s in range(planes):
+        collect(0, 0, s)
+    query_labels = labels_of(0)
+    lowest = jnp.full((8, query_count), -1.0, jnp.float32)
+    best = lowest
+    for s in range(last):
+        for m in range(near):
+            wait_recv(across(m, s))
+        for n, j in ((1, 1), (2, 2), (3, near + 1)):
+            collect(n, j, s)
+        if s < last - 1:
+            best = own_group(best, s, query_labels)
+    forward(last)
+    for n, j in ((1, 1), (2, 2)):
+        collect(n, j, last)
+
+    def cross(n, block, j):
+        columns = [labs[s, :, 0, :].T[:CAP, j : j + 1] for s in range(planes)]
+        found = compare(lowest, queries[block], columns, queries[n + 1], labels_of(n + 1), None)
+        cross_send[n] = jnp.max(found, axis=0, keepdims=True)
+        cross_copy(n).start()
+
+    best = own_group(best, last - 1, query_labels)
+    for m in range(near):
+        wait_recv(across(m, last))
+    collect(3, near + 1, last)
+    cross(0, 2, 2)
+    cross(1, 3, near + 1)
+    best = own_group(best, last, query_labels)
     best = jnp.max(best, axis=0, keepdims=True)
+    for n in range(2):
+        cross_copy(n).wait_recv()
+    best = jnp.maximum(best, jnp.maximum(cross_box[0], cross_box[1]))
     for n in range(planes // 2):
         best_send[n] = best[:, n * 128 : (n + 1) * 128]
     best_box[0] = best[:, :128]
@@ -327,13 +365,15 @@
     odd = lax.broadcasted_iota(jnp.int32, (8, docs), 0) % 2 == 1
     best_ref[...] = jnp.sum(jnp.where(member, jnp.where(odd, found[1], found[0]), 0.0), axis=0, keepdims=True)
 
+    for n in range(2):
+        cross_copy(n).wait_send()
     for d in range(1, planes):
         wait_send(along_z(d))
         best_copy(d).wait_send()
     for s in range(planes):
         for n in range(4):
             wait_send(hop(n, s))
-        for m in range(rows):
+        for m in range(near):
             wait_send(across(m, s))
     for peer in peers:
         hist_copy(*peer).wait()
@@ -345,6 +385,7 @@
     planes = cols // CORES
     docs, width = embeddings.shape
     blocks = CORES * rows
+    near = rows - 1
     hbm, vmem = pl.BlockSpec(memory_space=pl.ANY), pl.BlockSpec(memory_space=pltpu.VMEM)
     dma = pltpu.SemaphoreType.DMA
     row = lambda *lead: pltpu.VMEM((*lead, 1, 128), jnp.float32)
@@ -356,19 +397,22 @@
         scratch_shapes=[
             pltpu.VMEM((docs, width), jnp.bfloat16),
             pltpu.VMEM((1, docs), jnp.int32),
-            pltpu.VMEM((planes, blocks, CAP, width), jnp.bfloat16),
+            pltpu.VMEM((planes, CORES * near, CAP, width), jnp.bfloat16),
             pltpu.VMEM((planes - 1, CAP, width), jnp.bfloat16),
-            pltpu.VMEM((planes * CAP, width), jnp.bfloat16),
+            pltpu.VMEM((4, planes * CAP, width), jnp.bfloat16),
             row(planes - 1),
-            row(planes, blocks),
+            row(planes, 8),
+            pltpu.VMEM((2, 1, planes * CAP), jnp.float32),
+            pltpu.VMEM((2, 1, planes * CAP), jnp.float32),
             row(planes // 2),
             row(planes),
             row(),
             row(planes, blocks),
             dma((2,)),
-            dma((2, 2, planes)),
+            dma((2, 3, planes)),
             dma((2, 4, 2, planes)),
-            dma((2, rows, 2, planes)),
+            dma((2, near, 2, planes)),
+            dma((2, 2)),
             dma((2, planes)),
             dma((2, planes, blocks)),
         ],

time: 36.9 us -> 33.1 us (0.90)
  Pallas kernels: 35.1 us -> 31.3 us
    pallas_call x1, Pallas kernels: 35.1 us -> 31.3 us  [plane_shards(): pl.pallas_call(functools.partial(plane_kernel, planes, docs * rows * cols...]
where the time goes in v3:
time: 33.1 us; the launch traced here: 32.9 us
  Pallas kernels  31.3 us (95%)
  local copies, waits for them, and re-layouts  1.02 us (3%)
  between operations  0.64 us (2%)
    pallas_call x1, Pallas kernels, plane_shards(): pl.pallas_call(functools.partial(plane_kernel, planes, docs * rows * cols...  31.3 us
    unnamed x2, local copies, waits for them, and re-layouts  1.02 us

profile of v3, /device:TPU:0, one launch (start us, length us, event | category | flops | bytes accessed | tf_op | source)
XLA Modules:
  0.0 32.9 jit_solution(14837472103721078935)
XLA Ops:
  0.6 31.3 %shard_map.41 = (f32[1,128]{1,0:T(1,128)S(1)}, f32[1,128]{1,0:T(1,128)S(1)}) custom-call(bf16[128,768]{1,0:T(8,128)(2,1)} %emb_hbm.1, s32[1,128]{1,0:T(1,128)} %bitcast.5), custom_call_target="tpu_custom_call" | custom-call | tf_op jit(solution)/shard_map/pallas_call | solution.py:392
  31.9 0.5 %copy.6 = f32[128]{0:T(128)} copy(f32[128]{0:T(128)S(1)} %bitcast.4) | data formatting | bytes 1024
  32.4 0.5 %copy.7 = f32[128]{0:T(128)} copy(f32[128]{0:T(128)S(1)} %bitcast.3) | data formatting | bytes 1024
